TPU v7x, 32 devices: a whole 2x2x4 slice. The times are simulated.
32 devices in a mesh: rep: 4 (over z), shard: 8 (over y, x, core).
Axes of the slice: x: 2, y: 2, z: 4, core: 2. Of those that a mesh axis runs over, the one named last changes fastest.
Arguments:
- hidden_in: bfloat16 [8192, 2048], P(('rep', 'shard')), may hold values from -6 to 6
- cotangent: bfloat16 [8192, 2048], P(('rep', 'shard')), may hold values from -6 to 6
- lengths: int32 [32, 4], P(('rep', 'shard')), may hold values from 0 to 256, as said below
- offsets: int32 [32, 4], P(('rep', 'shard')), may hold values from 0 to 256, as said below
- projection_weight: bfloat16 [2048, 4096], P('shard'), may hold values from -0.125 to 0.125
- merge_weight: bfloat16 [2048, 2048], P('shard'), may hold values from -1 to 1
- expand_weight: bfloat16 [2048, 12288], P('shard'), may hold values from -0.125 to 0.125
- down_weight: bfloat16 [6144, 2048], P('shard'), may hold values from -0.078125 to 0.078125
- first_gain: bfloat16 [2048], P('shard'), may hold values from 0.099609375 to 1.8984375
- second_gain: bfloat16 [2048], P('shard'), may hold values from 0.099609375 to 1.8984375
- query_norm_scale: bfloat16 [128], P('shard'), may hold values from 0.099609375 to 1.8984375
- key_gain: bfloat16 [128], P('shard'), may hold values from 0.099609375 to 1.8984375
Outputs:
- output: bfloat16 [8192, 2048], P(('rep', 'shard'))
- input_grad: bfloat16 [8192, 2048], P(('rep', 'shard'))
- heads_grad: float32 [2048, 4096], P('shard')
- merge_grad: float32 [2048, 2048], P('shard')
- expand_grad: float32 [2048, 12288], P('shard')
- down_grad: float32 [6144, 2048], P('shard')
- first_grad: float32 [2048], P('shard')
- second_grad: float32 [2048], P('shard')
- query_grad: float32 [128], P('shard')
- key_grad: float32 [128], P('shard')
Inputs may be any that keep to these rules, and one draw needn't show every extreme that they name: `lengths`: row r belongs to device row r over rep+shard (rep the slower). An entry with length l > 0 and offset o holds one sequence in slots o to o + l - 1 of that device's 256 slots, with o + l <= 256; entries of a row never intersect; length 0 marks an empty entry. Some device holds one sequence of 256 tokens. `offsets`: first slot of each entry of lengths.
All inputs are finite; a program needn't handle non-finite values.
Results may differ from a plain program's by a relative error of at most 0.018.
Values may be sent and summed in bfloat16 or wider, within the bound.
No kernel may reach another device: no remote copies, remote signals or barrier semaphores. Data moves between devices by JAX's collectives and lax.ppermute only.
A program may use at most 448 MiB of HBM per device.

v0:
```python
import math
import jax
import jax.numpy as jnp
from jax import lax
from jax.sharding import PartitionSpec as P

QUERY_HEADS = 16
KEY_VALUE_HEADS = 8
HEAD_SIZE = 128
FF = 6144
EPS = 1e-06
THETA = 1000000.0
NEGATIVE = -1e30


def layout(lengths, offsets, slot_count):
    slots = jnp.arange(slot_count, dtype=jnp.int32)
    inside = (slots[:, None] >= offsets[None, :]) & (
        slots[:, None] < offsets[None, :] + lengths[None, :]
    )
    number = jnp.arange(lengths.shape[0], dtype=jnp.int32) + 1
    segment = jnp.sum(jnp.where(inside, number[None, :], 0), axis=1) - 1
    position = jnp.sum(jnp.where(inside, slots[:, None] - offsets[None, :], 0), axis=1)
    earlier = slots[None, :] <= slots[:, None]
    allowed = (segment[:, None] == segment[None, :]) & (segment[:, None] >= 0) & earlier
    allowed = allowed | (slots[None, :] == slots[:, None])
    expo = jnp.arange(HEAD_SIZE // 2, dtype=jnp.float32) * (2.0 / HEAD_SIZE)
    freq = jnp.power(THETA, -expo)
    angles = position.astype(jnp.float32)[:, None] * freq[None, :]
    return (allowed, jnp.cos(angles), jnp.sin(angles))


def apply_rotation(heads, cosine_table, sine_table):
    half = heads.shape[-1] // 2
    first = heads[..., :half]
    second = heads[..., half:]
    cosine_table = cosine_table[:, None, :]
    sine_table = sine_table[:, None, :]
    return jnp.concatenate(
        [first * cosine_table - second * sine_table, second * cosine_table + first * sine_table],
        axis=-1,
    )


def unrotate(grads, cosine_table, sine_table):
    half = grads.shape[-1] // 2
    first = grads[..., :half]
    second = grads[..., half:]
    cosine_table = cosine_table[:, None, :]
    sine_table = sine_table[:, None, :]
    return jnp.concatenate(
        [first * cosine_table + second * sine_table, second * cosine_table - first * sine_table],
        axis=-1,
    )


def norm_back(grads, unit, inverse, gain):
    scaled = grads * gain
    return inverse * (scaled - unit * jnp.mean(scaled * unit, axis=-1, keepdims=True))


def times_transposed(left, right):
    return lax.dot_general(
        left, right, (((1,), (1,)), ((), ())), preferred_element_type=jnp.float32
    )


def owner_rows(left, right):
    return lax.psum_scatter(
        lax.dot_general(
            left, right, (((0,), (0,)), ((), ())), preferred_element_type=jnp.float32
        ).astype(jnp.bfloat16),
        "shard",
        scatter_dimension=0,
        tiled=True,
    ).astype(jnp.float32)


def shards(
    hidden_in,
    cotangent,
    lengths,
    offsets,
    projection_weight,
    merge_weight,
    expand_weight,
    down_weight,
    first_gain,
    second_gain,
    query_norm_scale,
    key_gain,
):
    token_count = hidden_in.shape[0]
    head_group = QUERY_HEADS // KEY_VALUE_HEADS
    query_span = QUERY_HEADS * HEAD_SIZE
    key_span = KEY_VALUE_HEADS * HEAD_SIZE
    scale = 1.0 / math.sqrt(HEAD_SIZE)
    allowed, cosine_table, sine_table = layout(lengths[0], offsets[0], token_count)
    heads_full, merge_full, first_full, query_full, key_full = (
        lax.all_gather(projection_weight, "shard", axis=0, tiled=True),
        lax.all_gather(merge_weight, "shard", axis=0, tiled=True),
        lax.all_gather(first_gain, "shard", axis=0, tiled=True),
        lax.all_gather(query_norm_scale, "shard", axis=0, tiled=True),
        lax.all_gather(key_gain, "shard", axis=0, tiled=True),
    )
    first_scale = first_full.astype(jnp.float32)
    query_scale = query_full.astype(jnp.float32)
    key_scale = key_full.astype(jnp.float32)
    tokens = hidden_in.astype(jnp.float32)
    inverse_first = lax.rsqrt(jnp.mean(tokens * tokens, axis=1, keepdims=True) + EPS)
    unit_first = tokens * inverse_first
    normed = (unit_first * first_scale).astype(jnp.bfloat16)
    combined_projection = jnp.dot(normed, heads_full, preferred_element_type=jnp.float32)
    query_rows = combined_projection[:, :query_span].reshape(token_count, QUERY_HEADS, HEAD_SIZE)
    key_rows = combined_projection[:, query_span : query_span + key_span].reshape(
        token_count, KEY_VALUE_HEADS, HEAD_SIZE
    )
    value_rows = (
        combined_projection[:, query_span + key_span :]
        .reshape(token_count, KEY_VALUE_HEADS, HEAD_SIZE)
        .astype(jnp.bfloat16)
    )
    query_inverse = lax.rsqrt(jnp.mean(query_rows * query_rows, axis=-1, keepdims=True) + EPS)
    query_unit = query_rows * query_inverse
    key_inverse = lax.rsqrt(jnp.mean(key_rows * key_rows, axis=-1, keepdims=True) + EPS)
    key_unit = key_rows * key_inverse
    query_rotated = (
        apply_rotation(query_unit * query_scale, cosine_table, sine_table)
        .astype(jnp.bfloat16)
        .reshape(token_count, KEY_VALUE_HEADS, head_group, HEAD_SIZE)
    )
    key_rot = apply_rotation(key_unit * key_scale, cosine_table, sine_table).astype(jnp.bfloat16)
    scores = (
        jnp.einsum("qhgd,khd->hgqk", query_rotated, key_rot, preferred_element_type=jnp.float32)
        * scale
    )
    masked = jnp.where(allowed, scores, NEGATIVE)
    top = jnp.max(masked, axis=-1, keepdims=True)
    weights = jnp.where(allowed, jnp.exp(masked - top), 0.0)
    total = jnp.sum(weights, axis=-1, keepdims=True)
    logsum = top + jnp.log(total)
    probs = (weights / total).astype(jnp.bfloat16)
    context = jnp.einsum("hgqk,khd->qhgd", probs, value_rows, preferred_element_type=jnp.float32)
    context = context.reshape(token_count, query_span).astype(jnp.bfloat16)
    middle = tokens + jnp.dot(context, merge_full, preferred_element_type=jnp.float32)
    expand_full, down_full, second_full = (
        lax.all_gather(expand_weight, "shard", axis=0, tiled=True),
        lax.all_gather(down_weight, "shard", axis=0, tiled=True),
        lax.all_gather(second_gain, "shard", axis=0, tiled=True),
    )
    second_scale = second_full.astype(jnp.float32)
    inverse_second = lax.rsqrt(jnp.mean(middle * middle, axis=1, keepdims=True) + EPS)
    unit_second = middle * inverse_second
    normed_second = (unit_second * second_scale).astype(jnp.bfloat16)
    expanded = jnp.dot(normed_second, expand_full, preferred_element_type=jnp.float32)
    gates = expanded[:, :FF]
    ups = expanded[:, FF:]
    sigmoid = jax.nn.sigmoid(gates)
    activated = gates * sigmoid
    hidden = (activated * ups).astype(jnp.bfloat16)
    output = (middle + jnp.dot(hidden, down_full, preferred_element_type=jnp.float32)).astype(
        jnp.bfloat16
    )
    expand_back, down_back = (
        lax.all_gather(expand_weight, "shard", axis=0, tiled=True),
        lax.all_gather(down_weight, "shard", axis=0, tiled=True),
    )
    hidden_grad = times_transposed(cotangent, down_back)
    gate_grad = hidden_grad * ups * (sigmoid * (1.0 + gates * (1.0 - sigmoid)))
    up_grad = hidden_grad * activated
    expand_rows = jnp.concatenate([gate_grad, up_grad], axis=1).astype(jnp.bfloat16)
    second_back = times_transposed(expand_rows, expand_back)
    second_term = jnp.sum(second_back * unit_second, axis=0)
    middle_grad = cotangent.astype(jnp.float32) + norm_back(
        second_back, unit_second, inverse_second, second_scale
    )
    attention_rows = middle_grad.astype(jnp.bfloat16)
    heads_back, merge_back = (
        lax.all_gather(projection_weight, "shard", axis=0, tiled=True),
        lax.all_gather(merge_weight, "shard", axis=0, tiled=True),
    )
    context_grad = (
        times_transposed(attention_rows, merge_back)
        .astype(jnp.bfloat16)
        .reshape(token_count, KEY_VALUE_HEADS, head_group, HEAD_SIZE)
    )
    again_scores = (
        jnp.einsum("qhgd,khd->hgqk", query_rotated, key_rot, preferred_element_type=jnp.float32)
        * scale
    )
    probs_full = jnp.where(allowed, jnp.exp(again_scores - logsum), 0.0)
    probs_again = probs_full.astype(jnp.bfloat16)
    value_grad = jnp.einsum(
        "hgqk,qhgd->khd", probs_again, context_grad, preferred_element_type=jnp.float32
    )
    probs_grad = jnp.einsum(
        "qhgd,khd->hgqk", context_grad, value_rows, preferred_element_type=jnp.float32
    )
    delta = jnp.sum(probs_full * probs_grad, axis=-1, keepdims=True)
    score_grad = (probs_full * (probs_grad - delta)).astype(jnp.bfloat16)
    query_rot_grad = (
        jnp.einsum(
            "hgqk,khd->qhgd", score_grad, key_rot, preferred_element_type=jnp.float32
        ).reshape(token_count, QUERY_HEADS, HEAD_SIZE)
        * scale
    )
    key_rot_grad = (
        jnp.einsum("hgqk,qhgd->khd", score_grad, query_rotated, preferred_element_type=jnp.float32)
        * scale
    )
    query_normed_grad = unrotate(query_rot_grad, cosine_table, sine_table)
    key_normed_grad = unrotate(key_rot_grad, cosine_table, sine_table)
    query_term = jnp.sum(query_normed_grad * query_unit, axis=(0, 1))
    key_term = jnp.sum(key_normed_grad * key_unit, axis=(0, 1))
    query_back = norm_back(query_normed_grad, query_unit, query_inverse, query_scale)
    key_back = norm_back(key_normed_grad, key_unit, key_inverse, key_scale)
    united_rows = jnp.concatenate(
        [
            query_back.reshape(token_count, query_span),
            key_back.reshape(token_count, key_span),
            value_grad.reshape(token_count, key_span),
        ],
        axis=1,
    ).astype(jnp.bfloat16)
    first_back = times_transposed(united_rows, heads_back)
    first_term = jnp.sum(first_back * unit_first, axis=0)
    input_grad = (
        middle_grad + norm_back(first_back, unit_first, inverse_first, first_scale)
    ).astype(jnp.bfloat16)
    first_sum, second_sum, query_sum, key_sum = lax.psum(
        (first_term, second_term, query_term, key_term), ("rep", "shard")
    )
    index = lax.axis_index("shard")
    first_grad = lax.dynamic_slice_in_dim(
        first_sum, index * first_gain.shape[0], first_gain.shape[0]
    )
    second_grad = lax.dynamic_slice_in_dim(
        second_sum, index * second_gain.shape[0], second_gain.shape[0]
    )
    query_grad = lax.dynamic_slice_in_dim(
        query_sum, index * query_norm_scale.shape[0], query_norm_scale.shape[0]
    )
    key_grad = lax.dynamic_slice_in_dim(key_sum, index * key_gain.shape[0], key_gain.shape[0])
    heads_share = owner_rows(normed, united_rows)
    merge_share = owner_rows(context, attention_rows)
    expand_share = owner_rows(normed_second, expand_rows)
    down_share = owner_rows(hidden, cotangent)
    heads_grad, merge_grad, expand_grad, down_grad = (
        lax.psum(heads_share.astype(jnp.bfloat16), "rep").astype(jnp.float32),
        lax.psum(merge_share.astype(jnp.bfloat16), "rep").astype(jnp.float32),
        lax.psum(expand_share.astype(jnp.bfloat16), "rep").astype(jnp.float32),
        lax.psum(down_share.astype(jnp.bfloat16), "rep").astype(jnp.float32),
    )
    return (
        output,
        input_grad,
        heads_grad,
        merge_grad,
        expand_grad,
        down_grad,
        first_grad,
        second_grad,
        query_grad,
        key_grad,
    )


def solution(mesh):
    placed = (
        P(("rep", "shard"), None),
        P(("rep", "shard"), None),
        P(("rep", "shard"), None),
        P(("rep", "shard"), None),
        P("shard", None),
        P("shard", None),
        P("shard", None),
        P("shard", None),
        P("shard"),
        P("shard"),
        P("shard"),
        P("shard"),
    )
    return jax.shard_map(
        shards,
        mesh=mesh,
        in_specs=placed,
        out_specs=(
            P(("rep", "shard"), None),
            P(("rep", "shard"), None),
            P("shard", None),
            P("shard", None),
            P("shard", None),
            P("shard", None),
            P("shard"),
            P("shard"),
            P("shard"),
            P("shard"),
        ),
        check_vma=False,
    )
```

profile of v0, /device:TPU:0, one launch (start us, length us, event | category | flops | bytes accessed | tf_op | source)
XLA Modules:
  0.0 1668.1 jit_solution(12764290787771420811)
XLA Ops:
  8.0 0.7 all-gather.9.cloned.1.call-update
  8.7 0.7 all-gather.11.cloned.1.call-update
  10.1 10.4 all-gather
  22.4 14.2 all-reduce.4
  37.7 9.2 all-gather.1
  47.2 0.8 fusion.60
  48.5 54.0 %all-gather.7.cloned.1.call-done = bf16[2048,4096]{1,0:T(8,128)(2,1)} async-done(((bf16[256,4096]{1,0:T(8,128)(2,1)}), bf16[2048,4096]{1,0:T(8,128)(2,1)}) %all-gather.7.cloned.1.call-update) | async-done | bytes 16777232 | tf_op jit(solution)/shard_map/all_gather | solution.py:100
  102.5 8.2 fusion.57
  110.7 1.5 slice_bitcast_fusion.2
  113.5 1.8 slice_bitcast_fusion
  116.4 1.1 multiply_multiply_fusion
  117.5 0.8 subtract_convert_fusion
  118.8 2.1 fusion.49
  122.9 1.5 fusion.7
  124.4 1.0 fusion.12
  125.5 0.9 copy-done
  126.4 2.4 fusion.34
  128.8 29.9 %all-gather.9.cloned.1.call-done = bf16[2048,2048]{1,0:T(8,128)(2,1)} async-done(((bf16[256,2048]{1,0:T(8,128)(2,1)}), bf16[2048,2048]{1,0:T(8,128)(2,1)}) %all-gather.9.cloned.1.call-update) | async-done | bytes 8388624 | tf_op jit(solution)/shard_map/all_gather | solution.py:101
  158.7 7.4 multiply_reduce_fusion.3
  166.1 226.6 %all-gather.11.cloned.1.call-done = bf16[2048,12288]{1,0:T(8,128)(2,1)} async-done(((bf16[256,12288]{1,0:T(8,128)(2,1)}), bf16[2048,12288]{1,0:T(8,128)(2,1)}) %all-gather.11.cloned.1.call-update) | async-done | bytes 50331664 | tf_op jit(solution)/shard_map/all_gather | solution.py:147
  392.7 27.1 %fusion.75 = f32[256,12288]{1,0:T(8,128)} fusion(bf16[2048,12288]{1,0:T(8,128)(2,1)} %all-gather.11.cloned.1.call-done, f32[256,2048]{1,0:T(8,128)} %get-tuple-element.54, f32[2048]{0:T(1024)S(1)} %bitcast.201, f32[256]{0:T(256)S(1)} %add_rsqrt_fusion.2), kind=kOutput, calls=%fused_computation.152 | convolution fusion | flops 12886474752 | bytes 65020928 | tf_op jit(solution)/shard_map/dot_general | solution.py:155
  419.8 99.9 %all-gather.13.cloned.1.call-done = bf16[6144,2048]{1,0:T(8,128)(2,1)} async-done(((bf16[768,2048]{1,0:T(8,128)(2,1)}), bf16[6144,2048]{1,0:T(8,128)(2,1)}) %all-gather.13.cloned.1.call-update) | async-done | bytes 25165840 | tf_op jit(solution)/shard_map/all_gather | solution.py:148
  519.7 20.5 %multiply_convert_fusion.1 = (bf16[256,6144]{1,0:T(8,128)(2,1)}, bf16[256,6144]{1,0:T(8,128)(2,1)}, bf16[256,6144]{1,0:T(8,128)(2,1)}) fusion(f32[256,12288]{1,0:T(8,128)} %fusion.75, bf16[256,2048]{1,0:T(8,128)(2,1)} %param.13, bf16[6144,2048]{1,0:T(8,128)(2,1)} %all-gather.13.cloned.1.call-done), kind=kOutput, calls=%fused_computation.6 | convolution fusion | flops 6466043904 | bytes 48234496 | tf_op jit(solution)/shard_map/dot_general | solution.py:63
  540.2 24.4 %multiply_reduce_fusion = (f32[2048]{0:T(1024)}, f32[256]{0:T(256)S(1)}, f32[256,2048]{1,0:T(8,128)}) fusion(f32[256,2048]{1,0:T(8,128)} %get-tuple-element.54, f32[256]{0:T(256)S(1)} %add_rsqrt_fusion.2, f32[2048]{0:T(1024)S(1)} %bitcast.202, bf16[2048,12288]{1,0:T(8,128)(2,1)} %all-gather.11.cloned.1.call-done, bf16[256,6144]{1,0:T(8,128)(2,1)} %get-tuple-element.29, ...), kind=kOutput, calls=%fused_computation.54 | convolution fusion | flops 12900628480 | bytes 60835840 | tf_op jit(solution)/shard_map/dot_general | solution.py:63
  564.6 3.2 multiply_add_fusion.1
  567.8 1.3 copy-done.4
  569.1 5.7 convolution_convert_fusion.3
  575.6 1.2 broadcast_bitcast_fusion
  576.9 1.5 copy.148
  578.3 1.3 log_add_fusion
  579.7 8.8 convolution_convert_fusion.4
  588.5 2.6 copy.149
  591.1 4.3 fusion.1
  595.5 1.2 fusion.3
  596.7 0.8 convolution_multiply_fusion
  598.0 1.5 fusion.76
  599.5 3.9 copy.146
  603.5 3.7 copy.147
  607.1 3.1 fusion.39
  611.5 1.6 fusion.55
  613.6 1.5 copy.123
  615.1 4.4 fusion.40
  619.5 2.0 copy.145
  621.5 2.7 multiply_add_fusion
  624.3 2.1 multiply_reduce_fusion.1
  627.7 0.7 fusion.46
  629.6 3.3 fusion.28
  633.0 8.6 convolution_convert_fusion.2
  641.7 1.1 copy-done.18
  642.9 14.2 convolution_convert_fusion.1
  657.1 2.0 copy-done.3
  659.1 26.9 %convolution_convert_fusion = bf16[2048,12288]{1,0:T(8,128)(2,1)} fusion(bf16[256,6144]{1,0:T(8,128)(2,1)} %get-tuple-element.29, bf16[256,6144]{1,0:T(8,128)(2,1)} %get-tuple-element.28, f32[256,2048]{1,0:T(8,128)S(1)} %copy-done.3, f32[2048]{0:T(1024)S(1)} %bitcast.204, f32[256]{0:T(256)S(1)} %add_rsqrt_fusion.2), kind=kOutput, calls=%fused_computation | convolution fusion | flops 12924223488 | bytes 58729472 | tf_op jit(solution)/shard_map/dot_general | solution.py:70
  686.1 80.1 %reduce-scatter.7.cloned.1.call-done = bf16[256,4096]{1,0:T(8,128)(2,1)} async-done(((bf16[2048,4096]{1,0:T(8,128)(2,1)}), bf16[256,4096]{1,0:T(8,128)(2,1)}) %reduce-scatter.7.cloned.1.call-update) | async-done | bytes 2097168 | tf_op jit(solution)/shard_map/reduce_scatter | solution.py:69
  766.2 159.9 %reduce-scatter.11.cloned.1.call-done = bf16[768,2048]{1,0:T(8,128)(2,1)} async-done(((bf16[6144,2048]{1,0:T(8,128)(2,1)}), bf16[768,2048]{1,0:T(8,128)(2,1)}) %reduce-scatter.11.cloned.1.call-update) | async-done | bytes 3145744 | tf_op jit(solution)/shard_map/reduce_scatter | solution.py:69
  926.1 288.0 %reduce-scatter.13.cloned.1.call-done = bf16[256,12288]{1,0:T(8,128)(2,1)} async-done(((bf16[2048,12288]{1,0:T(8,128)(2,1)}), bf16[256,12288]{1,0:T(8,128)(2,1)}) %reduce-scatter.13.cloned.1.call-update) | async-done | bytes 6291472
  1214.2 12.6 fusion.23
  1226.8 45.0 %all-reduce.3 = (f32[2048]{0:T(1024)S(1)}, f32[2048]{0:T(1024)S(1)}, f32[128]{0:T(128)S(1)}, f32[128]{0:T(128)S(1)}) all-reduce(f32[2048]{0:T(1024)S(1)} %get-tuple-element.12, f32[2048]{0:T(1024)S(1)} %copy-done.41, f32[128]{0:T(128)S(1)} %bitcast_reduce_fusion, ...), channel_id=1, replica_groups=mesh['rep'=4,'shard'=8] {'rep','shard'}, use_global_device_ids=true, to_apply=%region_22.23 | all-reduce | flops 4352 | bytes 34816 | tf_op jit(solution)/shard_map/psum | solution.py:230
  1274.2 4.0 fusion.22
  1278.3 12.9 fusion.13
  1291.2 353.0 %all-reduce.8.cloned.1.call-done = (bf16[256,4096]{1,0:T(8,128)(2,1)}, bf16[256,2048]{1,0:T(8,128)(2,1)}, bf16[256,12288]{1,0:T(8,128)(2,1)}, bf16[768,2048]{1,0:T(8,128)(2,1)}) async-done(((bf16[256,4096]{1,0:T(8,128)(2,1)}, bf16[256,2048]{1,0:T(8,128)(2,1)}, bf16[256,12288]{1,0:T(8,128)(2,1)}, bf16[768,2048]{1,0:T(8,128)(2,1)}), (bf16[256,4096]{1,0:T(8,128)(2,1)}, bf16[256,2048]{1,0:T(8,128)(2,1)}, ...) | async-done | bytes 12582928 | tf_op jit(solution)/shard_map/psum | solution.py:249
  1644.2 9.2 convert_element_type.131
  1653.5 3.5 convert_element_type.133
  1657.0 2.5 convert_element_type.127
  1659.5 1.6 convert_element_type.129
  (169 shorter events, 17.5 us)
Async XLA Ops:
  7.2 95.3 %all-gather.7.cloned.1.call-start = ((), (), s32[]{:S(2)}) async-start(), calls=%async_computation.4 | async-start | bytes 18874368 | tf_op jit(solution)/shard_map/all_gather | solution.py:100
  7.9 150.8 %all-gather.9.cloned.1.call-start = ((), (), s32[]{:S(2)}) async-start(), calls=%async_computation.5 | async-start | bytes 9437184 | tf_op jit(solution)/shard_map/all_gather | solution.py:101
  8.7 384.1 %all-gather.11.cloned.1.call-start = ((), (), s32[]{:S(2)}) async-start(), calls=%async_computation.6 | async-start | bytes 56623104 | tf_op jit(solution)/shard_map/all_gather | solution.py:147
  9.4 0.7 copy-start.47
  9.4 11.2 copy-start.52
  9.4 12.4 copy-start.48
  9.4 12.7 copy-start.49
  9.4 27.6 %copy-start.46 = (s32[1,4]{1,0:T(1,128)S(1)}, s32[1,4]{1,0:T(1,128)}, u32[]{:S(2)}) copy-start(s32[1,4]{1,0:T(1,128)} %param.15) | copy-start | bytes 52
  9.4 27.6 %copy-start.50 = (s32[1,4]{1,0:T(1,128)S(1)}, s32[1,4]{1,0:T(1,128)}, u32[]{:S(2)}) copy-start(s32[1,4]{1,0:T(1,128)} %param.14) | copy-start | bytes 52
  9.5 28.2 %copy-start.51 = (bf16[256]{0:T(256)(128)(2,1)S(1)}, bf16[256]{0:T(256)(128)(2,1)}, u32[]{:S(2)}) copy-start(bf16[256]{0:T(256)(128)(2,1)} %param.21) | copy-start | bytes 1540
  9.5 37.4 %copy-start.2 = (bf16[256,2048]{1,0:T(8,128)(2,1)S(1)}, bf16[256,2048]{1,0:T(8,128)(2,1)}, u32[]{:S(2)}) copy-start(bf16[256,2048]{1,0:T(8,128)(2,1)} %param.12) | copy-start | bytes 3145732
  9.5 510.2 %all-gather.13.cloned.1.call-start = ((), (), s32[]{:S(2)}) async-start(), calls=%async_computation.7 | async-start | bytes 28311552 | tf_op jit(solution)/shard_map/all_gather | solution.py:148
  10.1 676.0 %reduce-scatter.9.cloned.1.call-start = ((), (), s32[]{:S(2)}) async-start(), calls=%async_computation.9 | async-start | bytes 9437184 | tf_op jit(solution)/shard_map/reduce_scatter | solution.py:69
  20.6 90.1 %copy-start.31 = (f32[8,1,256]{2,1,0:T(1,128)}, f32[8,1,256]{2,1,0:T(1,128)S(1)}, u32[]{:S(2)}) copy-start(f32[8,1,256]{2,1,0:T(1,128)S(1)} %convert_element_type.134) | copy-start | bytes 24580
  47.2 63.5 %copy-start.39 = (f32[256]{0:T(256)}, f32[256]{0:T(256)S(1)}, u32[]{:S(2)}) copy-start(f32[256]{0:T(256)S(1)} %add_rsqrt_fusion.3) | copy-start | bytes 3076
  110.7 2.3 copy-start.6
  115.7 0.7 copy-start.42
  118.5 4.0 copy-start.10
  118.5 3.2 copy-start.8
  118.5 3.2 copy-start.44
  118.8 3.7 copy-start.11
  121.0 4.4 copy-start.25
  121.0 0.6 copy-start.35
  122.0 0.8 copy-start.26
  122.5 1.9 copy-start.13
  122.5 1.9 copy-start.15
  124.4 2.0 copy-start
  124.4 2.0 copy-start.33
  125.4 1.0 copy-start.37
  564.6 4.5 copy-start.12
  567.8 1.3 copy-start.4
  574.9 191.3 %reduce-scatter.7.cloned.1.call-start = ((), (), s32[]{:S(2)}) async-start(), calls=%async_computation.8 | async-start | bytes 18874368 | tf_op jit(solution)/shard_map/reduce_scatter | solution.py:69
  591.1 4.4 copy-start.1
  591.1 4.4 copy-start.27
  591.1 4.4 copy-start.34
  595.5 1.2 copy-start.14
  595.5 1.2 copy-start.16
  596.7 1.3 copy-start.5
  610.2 1.2 copy-start.9
  610.2 1.2 copy-start.36
  610.2 1.2 copy-start.45
  621.5 2.7 copy-start.43
  624.2 2.2 copy-start.30
  624.2 2.5 copy-start.29
  624.2 2.9 copy-start.7
  626.4 1.3 copy-start.20
  628.4 4.6 copy-start.23
  628.4 1.2 copy-start.38
  629.6 3.4 copy-start.24
  629.6 3.4 copy-start.32
  629.6 3.4 copy-start.40
  632.9 8.7 copy-start.19
  641.6 1.2 copy-start.18
  641.7 284.5 %reduce-scatter.11.cloned.1.call-start = ((), (), s32[]{:S(2)}) async-start(), calls=%async_computation.10 | async-start | bytes 28311552 | tf_op jit(solution)/shard_map/reduce_scatter | solution.py:69
  657.0 2.0 copy-start.3
  657.0 557.1 %reduce-scatter.13.cloned.1.call-start = ((), (), s32[]{:S(2)}) async-start(), calls=%async_computation.11 | async-start | bytes 56623104
  686.0 958.2 %all-reduce.8.cloned.1.call-start = ((), (), s32[]{:S(2)}) async-start(), calls=%async_computation.12 | async-start | bytes 25165824 | tf_op jit(solution)/shard_map/psum | solution.py:249
  1214.2 12.6 copy-start.41
  1274.2 4.0 copy-start.17
  1644.2 9.2 copy-start.21
  1653.5 3.6 copy-start.22
  1657.0 2.5 copy-start.28
Sparse Core Ops, SparseCore 0:
  9.9 92.6 all-gather.6
  104.4 54.2 all-gather.8
  160.6 232.0 all-gather.10
  394.5 125.1 all-gather.12
  575.0 71.4 reduce-scatter.8
  650.0 116.1 reduce-scatter.6
  769.8 156.2 reduce-scatter.10
  929.8 284.3 reduce-scatter.12
  1217.0 427.1 all-reduce.7
where the time goes:
time: 1670 us
  waiting for transfers between devices  1290 us (77%)
  matrix products  194 us (12%)
  blocking collectives  78.8 us (5%)
  other arithmetic  45.5 us (3%)
  local copies, waits for them, and re-layouts  39.6 us (2%)
    psum x1, waiting for transfers between devices, shards(): lax.psum(heads_share.astype(jnp.bfloat16), 'rep').astype(jnp.float32)  353 us
    unnamed x10, waiting for transfers between devices  291 us
    reduce_scatter x3, waiting for transfers between devices, owner_rows(): lax.psum_scatter(lax.dot_general(left, right, (((0,), (0,)), ((), ())), p...  240 us
    all_gather x1, waiting for transfers between devices, shards(): lax.all_gather(expand_weight, 'shard', axis=0, tiled=True)  227 us
    all_gather x1, waiting for transfers between devices, shards(): lax.all_gather(down_weight, 'shard', axis=0, tiled=True)  99.9 us
    dot_general x4, matrix products, times_transposed(): lax.dot_general(left, right, (((1,), (1,)), ((), ())), preferred_element_...  66.3 us
    dot_general x4, matrix products, owner_rows(): lax.dot_general(left, right, (((0,), (0,)), ((), ())), preferred_element_...  55.5 us
    all_gather x1, waiting for transfers between devices, shards(): lax.all_gather(projection_weight, 'shard', axis=0, tiled=True)  54 us
  transfers between devices with their start and end apart: 9, of which 8 were waited for; matrix products, arithmetic and copies ran while one was open for 12% of the time, Pallas kernels for 0%

commit v1 on v0

--- a/solution.py
+++ b/solution.py
@@ -246,7 +246,9 @@
     expand_share = owner_rows(normed_second, expand_rows)
     down_share = owner_rows(hidden, cotangent)
     heads_grad, merge_grad, expand_grad, down_grad = (
-        lax.psum(heads_share.astype(jnp.bfloat16), "rep").astype(jnp.float32),
+        jnp.sum(lax.all_gather(heads_share.astype(jnp.bfloat16), "rep"), axis=0).astype(
+            jnp.float32
+        ),
         lax.psum(merge_share.astype(jnp.bfloat16), "rep").astype(jnp.float32),
         lax.psum(expand_share.astype(jnp.bfloat16), "rep").astype(jnp.float32),
         lax.psum(down_share.astype(jnp.bfloat16), "rep").astype(jnp.float32),

time: 1670 us -> 1810 us (1.084)
  waiting for transfers between devices: 1290 us -> 1420 us
    all_gather x0 -> x1, waiting for transfers between devices: none -> 72.2 us  [shards(): lax.all_gather(heads_share.astype(jnp.bfloat16), 'rep')]
    reduce_scatter x3, waiting for transfers between devices: 240 us -> 298 us  [owner_rows(): lax.psum_scatter(lax.dot_general(left, right, (((0,), (0,)), ((), ())), p...]
    unnamed x10 -> x11, waiting for transfers between devices: 291 us -> 291 us
  transfers between devices with their start and end apart: 9 -> 10, of which waited for: 8 -> 10; matrix products, arithmetic and copies ran while one was open for 12% -> 9% of each run, Pallas kernels for 0% -> 0%
where the time goes in v1:
time: 1810 us; the launch traced here: 1800 us
  waiting for transfers between devices  1420 us (78%)
  matrix products  190 us (10%)
  blocking collectives  81.9 us (5%)
  other arithmetic  52.4 us (3%)
  local copies, waits for them, and re-layouts  41.7 us (2%)
    psum x1, waiting for transfers between devices, shards(): lax.psum(merge_share.astype(jnp.bfloat16), 'rep').astype(jnp.float32)  352 us
    reduce_scatter x3, waiting for transfers between devices, owner_rows(): lax.psum_scatter(lax.dot_general(left, right, (((0,), (0,)), ((), ())), p...  298 us
    unnamed x11, waiting for transfers between devices  291 us
    all_gather x1, waiting for transfers between devices, shards(): lax.all_gather(expand_weight, 'shard', axis=0, tiled=True)  226 us
    all_gather x1, waiting for transfers between devices, shards(): lax.all_gather(down_weight, 'shard', axis=0, tiled=True)  99.8 us
    all_gather x1, waiting for transfers between devices, shards(): lax.all_gather(heads_share.astype(jnp.bfloat16), 'rep')  72.2 us
    dot_general x4, matrix products, times_transposed(): lax.dot_general(left, right, (((1,), (1,)), ((), ())), preferred_element_...  64.1 us
    dot_general x4, matrix products, owner_rows(): lax.dot_general(left, right, (((0,), (0,)), ((), ())), preferred_element_...  57.7 us
  transfers between devices with their start and end apart: 10, of which 10 were waited for; matrix products, arithmetic and copies ran while one was open for 9% of the time, Pallas kernels for 0%

profile of v1, /device:TPU:0, one launch (start us, length us, event | category | flops | bytes accessed | tf_op | source)
XLA Modules:
  0.0 1799.4 jit_solution(1155087046700060400)
XLA Ops:
  10.1 10.4 all-gather.1
  22.4 14.2 all-reduce.4
  36.7 9.2 all-gather.2
  48.7 53.9 %all-gather.9.cloned.1.call-done = bf16[2048,4096]{1,0:T(8,128)(2,1)} async-done(((bf16[256,4096]{1,0:T(8,128)(2,1)}), bf16[2048,4096]{1,0:T(8,128)(2,1)}) %all-gather.9.cloned.1.call-update) | async-done | bytes 16777232 | tf_op jit(solution)/shard_map/all_gather | solution.py:100
  102.6 8.2 fusion.57
  110.8 2.0 copy-done.6
  112.8 1.2 slice_bitcast_fusion.2
  115.3 1.7 slice_bitcast_fusion
  118.1 1.1 multiply_multiply_fusion
  119.9 1.2 copy.108
  121.2 1.2 copy.109
  122.4 1.3 fusion.49
  123.7 0.9 copy.152
  125.5 1.7 fusion.47
  127.7 1.5 fusion.7
  129.2 1.0 fusion.12
  130.3 0.9 copy-done
  131.2 2.4 fusion.34
  133.6 25.2 %all-gather.11.cloned.1.call-done = bf16[2048,2048]{1,0:T(8,128)(2,1)} async-done(((bf16[256,2048]{1,0:T(8,128)(2,1)}), bf16[2048,2048]{1,0:T(8,128)(2,1)}) %all-gather.11.cloned.1.call-update) | async-done | bytes 8388624 | tf_op jit(solution)/shard_map/all_gather | solution.py:101
  158.8 7.4 multiply_reduce_fusion.3
  166.9 226.0 %all-gather.13.cloned.1.call-done = bf16[2048,12288]{1,0:T(8,128)(2,1)} async-done(((bf16[256,12288]{1,0:T(8,128)(2,1)}), bf16[2048,12288]{1,0:T(8,128)(2,1)}) %all-gather.13.cloned.1.call-update) | async-done | bytes 50331664 | tf_op jit(solution)/shard_map/all_gather | solution.py:147
  392.8 27.1 %fusion.75 = f32[256,12288]{1,0:T(8,128)} fusion(bf16[2048,12288]{1,0:T(8,128)(2,1)} %all-gather.13.cloned.1.call-done, f32[256,2048]{1,0:T(8,128)} %get-tuple-element.53, f32[2048]{0:T(1024)S(1)} %bitcast.203, f32[256]{0:T(256)S(1)} %add_rsqrt_fusion.2), kind=kOutput, calls=%fused_computation.152 | convolution fusion | flops 12886474752 | bytes 65020928 | tf_op jit(solution)/shard_map/dot_general | solution.py:155
  420.0 99.8 %all-gather.15.cloned.1.call-done = bf16[6144,2048]{1,0:T(8,128)(2,1)} async-done(((bf16[768,2048]{1,0:T(8,128)(2,1)}), bf16[6144,2048]{1,0:T(8,128)(2,1)}) %all-gather.15.cloned.1.call-update) | async-done | bytes 25165840 | tf_op jit(solution)/shard_map/all_gather | solution.py:148
  519.8 20.4 %multiply_convert_fusion.1 = (bf16[256,6144]{1,0:T(8,128)(2,1)}, bf16[256,6144]{1,0:T(8,128)(2,1)}, bf16[256,6144]{1,0:T(8,128)(2,1)}) fusion(f32[256,12288]{1,0:T(8,128)} %fusion.75, bf16[256,2048]{1,0:T(8,128)(2,1)} %param.13, bf16[6144,2048]{1,0:T(8,128)(2,1)} %all-gather.15.cloned.1.call-done), kind=kOutput, calls=%fused_computation.6 | convolution fusion | flops 6466043904 | bytes 48234496 | tf_op jit(solution)/shard_map/dot_general | solution.py:63
  540.2 24.5 %multiply_reduce_fusion = (f32[2048]{0:T(1024)}, f32[256]{0:T(256)S(1)}, f32[256,2048]{1,0:T(8,128)}) fusion(f32[256,2048]{1,0:T(8,128)} %get-tuple-element.53, f32[256]{0:T(256)S(1)} %add_rsqrt_fusion.2, f32[2048]{0:T(1024)S(1)} %bitcast.204, bf16[2048,12288]{1,0:T(8,128)(2,1)} %all-gather.13.cloned.1.call-done, bf16[256,6144]{1,0:T(8,128)(2,1)} %get-tuple-element.28, ...), kind=kOutput, calls=%fused_computation.54 | convolution fusion | flops 12900628480 | bytes 60835840 | tf_op jit(solution)/shard_map/dot_general | solution.py:63
  564.7 3.1 multiply_add_fusion.1
  567.8 1.3 copy-done.4
  569.1 6.7 convolution_convert_fusion.4
  575.8 2.7 copy.149
  578.6 4.2 fusion.1
  582.8 1.2 fusion.3
  585.5 1.9 fusion.39
  587.4 1.8 fusion.40
  589.2 1.5 fusion.76
  590.6 3.7 copy.146
  594.3 3.7 copy.147
  598.0 2.7 multiply_add_fusion
  600.7 2.9 multiply_reduce_fusion.1
  605.0 1.6 fusion.55
  608.0 2.1 copy.145
  611.3 1.0 copy-done.7
  612.2 3.9 fusion.28
  617.8 8.6 convolution_convert_fusion.2
  626.5 1.5 copy-done.5
  628.0 7.3 convolution_convert_fusion.3
  635.4 1.4 copy-done.20
  636.8 18.2 %convolution_convert_fusion.1 = bf16[6144,2048]{1,0:T(8,128)(2,1)} fusion(bf16[256,6144]{1,0:T(8,128)(2,1)} %get-tuple-element.29, bf16[256,2048]{1,0:T(8,128)(2,1)S(1)} %copy-done.20), kind=kOutput, calls=%fused_computation.1 | convolution fusion | flops 6455033856 | bytes 29360128 | tf_op jit(solution)/shard_map/dot_general | solution.py:70
  655.1 1.5 copy-done.3
  656.6 23.7 %convolution_convert_fusion = bf16[2048,12288]{1,0:T(8,128)(2,1)} fusion(bf16[256,6144]{1,0:T(8,128)(2,1)} %get-tuple-element.28, bf16[256,6144]{1,0:T(8,128)(2,1)} %get-tuple-element.27, f32[256,2048]{1,0:T(8,128)S(1)} %copy-done.3, f32[2048]{0:T(1024)S(1)} %bitcast.206, f32[256]{0:T(256)S(1)} %add_rsqrt_fusion.2), kind=kOutput, calls=%fused_computation | convolution fusion | flops 12924223488 | bytes 58729472 | tf_op jit(solution)/shard_map/dot_general | solution.py:70
  680.3 62.5 %reduce-scatter.7.cloned.1.call-done = bf16[256,4096]{1,0:T(8,128)(2,1)} async-done(((bf16[2048,4096]{1,0:T(8,128)(2,1)}), bf16[256,4096]{1,0:T(8,128)(2,1)}) %reduce-scatter.7.cloned.1.call-update) | async-done | bytes 2097168 | tf_op jit(solution)/shard_map/reduce_scatter | solution.py:69
  742.8 75.4 %reduce-scatter.9.cloned.1.call-done = bf16[256,2048]{1,0:T(8,128)(2,1)} async-done(((bf16[2048,2048]{1,0:T(8,128)(2,1)}), bf16[256,2048]{1,0:T(8,128)(2,1)}) %reduce-scatter.9.cloned.1.call-update) | async-done | bytes 1048592 | tf_op jit(solution)/shard_map/reduce_scatter | solution.py:69
  818.2 159.9 %reduce-scatter.11.cloned.1.call-done = bf16[768,2048]{1,0:T(8,128)(2,1)} async-done(((bf16[6144,2048]{1,0:T(8,128)(2,1)}), bf16[768,2048]{1,0:T(8,128)(2,1)}) %reduce-scatter.11.cloned.1.call-update) | async-done | bytes 3145744 | tf_op jit(solution)/shard_map/reduce_scatter | solution.py:69
  978.2 288.0 %reduce-scatter.13.cloned.1.call-done = bf16[256,12288]{1,0:T(8,128)(2,1)} async-done(((bf16[2048,12288]{1,0:T(8,128)(2,1)}), bf16[256,12288]{1,0:T(8,128)(2,1)}) %reduce-scatter.13.cloned.1.call-update) | async-done | bytes 6291472
  1266.2 12.6 fusion.23
  1278.8 48.1 %all-reduce.3 = (f32[2048]{0:T(1024)S(1)}, f32[2048]{0:T(1024)S(1)}, f32[128]{0:T(128)S(1)}, f32[128]{0:T(128)S(1)}) all-reduce(f32[2048]{0:T(1024)S(1)} %get-tuple-element.12, f32[2048]{0:T(1024)S(1)} %copy-done.47, f32[128]{0:T(128)S(1)} %bitcast_reduce_fusion, ...), channel_id=1, replica_groups=mesh['rep'=4,'shard'=8] {'rep','shard'}, use_global_device_ids=true, to_apply=%region_22.23 | all-reduce | flops 4352 | bytes 34816 | tf_op jit(solution)/shard_map/psum | solution.py:230
  1329.4 4.0 fusion.22
  1333.3 12.9 fusion.13
  1346.2 72.2 %all-gather.17.cloned.1.call-done = bf16[1024,4096]{1,0:T(8,128)(2,1)} async-done(((bf16[256,4096]{1,0:T(8,128)(2,1)}), bf16[1024,4096]{1,0:T(8,128)(2,1)}) %all-gather.17.cloned.1.call-update) | async-done | bytes 8388624 | tf_op jit(solution)/shard_map/all_gather | solution.py:249
  1418.4 5.2 reduce_sum.182
  1423.6 2.7 convert_element_type.129
  1426.3 351.6 %all-reduce.8.cloned.1.call-done = (bf16[256,2048]{1,0:T(8,128)(2,1)}, bf16[256,12288]{1,0:T(8,128)(2,1)}, bf16[768,2048]{1,0:T(8,128)(2,1)}) async-done(((bf16[256,2048]{1,0:T(8,128)(2,1)}, bf16[256,12288]{1,0:T(8,128)(2,1)}, bf16[768,2048]{1,0:T(8,128)(2,1)}), (bf16[256,2048]{1,0:T(8,128)(2,1)}, bf16[256,12288]{1,0:T(8,128)(2,1)}, bf16[768,2048]{1,0:T(8,128)(2,1)})) %all-reduce.8.cloned.1.call-update) | async-done | bytes 10485776 | tf_op jit(solution)/shard_map/psum | solution.py:252
  1777.8 9.2 convert_element_type.133
  1787.0 3.5 convert_element_type.135
  1790.6 1.6 convert_element_type.131
  (185 shorter events, 21.6 us)
Async XLA Ops:
  7.2 95.4 %all-gather.9.cloned.1.call-start = ((), (), s32[]{:S(2)}) async-start(), calls=%async_computation.4 | async-start | bytes 18874368 | tf_op jit(solution)/shard_map/all_gather | solution.py:100
  7.9 150.9 %all-gather.11.cloned.1.call-start = ((), (), s32[]{:S(2)}) async-start(), calls=%async_computation.5 | async-start | bytes 9437184 | tf_op jit(solution)/shard_map/all_gather | solution.py:101
  8.7 384.2 %all-gather.13.cloned.1.call-start = ((), (), s32[]{:S(2)}) async-start(), calls=%async_computation.6 | async-start | bytes 56623104 | tf_op jit(solution)/shard_map/all_gather | solution.py:147
  9.4 11.2 copy-start.58
  9.4 12.4 copy-start.54
  9.4 12.7 copy-start.55
  9.4 27.1 %copy-start.52 = (s32[1,4]{1,0:T(1,128)S(1)}, s32[1,4]{1,0:T(1,128)}, u32[]{:S(2)}) copy-start(s32[1,4]{1,0:T(1,128)} %param.15) | copy-start | bytes 52
  9.4 27.1 %copy-start.56 = (s32[1,4]{1,0:T(1,128)S(1)}, s32[1,4]{1,0:T(1,128)}, u32[]{:S(2)}) copy-start(s32[1,4]{1,0:T(1,128)} %param.14) | copy-start | bytes 52
  9.5 27.2 %copy-start.57 = (bf16[256]{0:T(256)(128)(2,1)S(1)}, bf16[256]{0:T(256)(128)(2,1)}, u32[]{:S(2)}) copy-start(bf16[256]{0:T(256)(128)(2,1)} %param.21) | copy-start | bytes 1540
  9.5 36.5 %copy-start.2 = (bf16[256,2048]{1,0:T(8,128)(2,1)S(1)}, bf16[256,2048]{1,0:T(8,128)(2,1)}, u32[]{:S(2)}) copy-start(bf16[256,2048]{1,0:T(8,128)(2,1)} %param.12) | copy-start | bytes 3145732
  9.5 510.3 %all-gather.15.cloned.1.call-start = ((), (), s32[]{:S(2)}) async-start(), calls=%async_computation.7 | async-start | bytes 28311552 | tf_op jit(solution)/shard_map/all_gather | solution.py:148
  10.1 732.7 %reduce-scatter.7.cloned.1.call-start = ((), (), s32[]{:S(2)}) async-start(), calls=%async_computation.8 | async-start | bytes 18874368 | tf_op jit(solution)/shard_map/reduce_scatter | solution.py:69
  20.6 90.2 %copy-start.33 = (f32[8,1,256]{2,1,0:T(1,128)}, f32[8,1,256]{2,1,0:T(1,128)S(1)}, u32[]{:S(2)}) copy-start(f32[8,1,256]{2,1,0:T(1,128)S(1)} %convert_element_type.136) | copy-start | bytes 24580
  36.5 74.3 %copy-start.48 = (f32[128]{0:T(128)}, f32[128]{0:T(128)S(1)}, u32[]{:S(2)}) copy-start(f32[128]{0:T(128)S(1)} %convert_element_type.111) | copy-start | bytes 1540
  36.7 81.4 %copy-start.50 = (f32[128]{0:T(128)}, f32[128]{0:T(128)S(1)}, u32[]{:S(2)}) copy-start(f32[128]{0:T(128)S(1)} %convert_element_type.113) | copy-start | bytes 1540
  46.3 64.5 %copy-start.44 = (f32[256]{0:T(256)}, f32[256]{0:T(256)S(1)}, u32[]{:S(2)}) copy-start(f32[256]{0:T(256)S(1)} %add_rsqrt_fusion.3) | copy-start | bytes 3076
  110.8 2.0 copy-start.6
  119.9 4.7 copy-start.43
  124.7 4.5 copy-start.38
  125.5 2.2 copy-start.9
  125.5 2.2 copy-start.11
  125.5 2.2 copy-start.28
  127.6 1.6 copy-start.15
  127.6 1.6 copy-start.17
  129.2 2.0 copy-start
  129.2 2.0 copy-start.36
  129.2 2.0 copy-start.27
  158.8 7.4 copy-start.37
  158.8 7.4 copy-start.41
  567.8 1.3 copy-start.4
  578.5 4.2 copy-start.1
  578.5 4.2 copy-start.29
  578.5 4.2 copy-start.35
  584.0 1.5 copy-start.12
  585.5 1.9 copy-start.22
  598.0 2.7 copy-start.51
  600.7 3.7 copy-start.13
  603.7 1.3 copy-start.8
  603.7 1.3 copy-start.39
  603.7 1.3 copy-start.49
  604.9 5.1 copy-start.32
  605.0 6.3 copy-start.14
  610.0 2.2 copy-start.7
  610.0 2.2 copy-start.42
  612.2 4.3 copy-start.31
  612.2 4.6 copy-start.23
  612.2 4.6 copy-start.46
  616.5 1.2 copy-start.21
  616.5 1.4 copy-start.26
  616.5 1.3 copy-start.34
  616.5 1.3 copy-start.45
  617.6 8.9 copy-start.25
  626.4 1.6 copy-start.5
  626.5 191.7 %reduce-scatter.9.cloned.1.call-start = ((), (), s32[]{:S(2)}) async-start(), calls=%async_computation.9 | async-start | bytes 9437184 | tf_op jit(solution)/shard_map/reduce_scatter | solution.py:69
  635.3 1.5 copy-start.20
  635.3 342.8 %reduce-scatter.11.cloned.1.call-start = ((), (), s32[]{:S(2)}) async-start(), calls=%async_computation.10 | async-start | bytes 28311552 | tf_op jit(solution)/shard_map/reduce_scatter | solution.py:69
  655.0 1.6 copy-start.3
  655.0 611.1 %reduce-scatter.13.cloned.1.call-start = ((), (), s32[]{:S(2)}) async-start(), calls=%async_computation.12 | async-start | bytes 56623104
  680.3 738.1 %all-gather.17.cloned.1.call-start = ((), (), s32[]{:S(2)}) async-start(), calls=%async_computation.11 | async-start | bytes 10485760 | tf_op jit(solution)/shard_map/all_gather | solution.py:249
  742.8 1035.0 %all-reduce.8.cloned.1.call-start = ((), (), s32[]{:S(2)}) async-start(), calls=%async_computation.13 | async-start | bytes 20971520 | tf_op jit(solution)/shard_map/psum | solution.py:252
  1266.2 12.6 copy-start.47
  1329.4 4.0 copy-start.19
  1777.8 9.2 copy-start.24
  1787.0 3.6 copy-start.30
  (5 other events, 5.3 us)
Sparse Core Ops, SparseCore 0:
  9.9 92.6 all-gather.8
  104.5 54.2 all-gather.10
  160.7 232.0 all-gather.12
  394.6 125.1 all-gather.14
  626.6 116.1 reduce-scatter.6
  746.7 71.5 reduce-scatter.8
  821.8 156.2 reduce-scatter.10
  981.8 284.3 reduce-scatter.12
  1267.7 150.6 all-gather.16
  1421.1 356.7 all-reduce.7
